TPU v7x, 256 devices: a whole 4x4x8 slice. The times are simulated.
256 devices in a mesh: replica: 8 (over z_lo, x), fsdp: 32 (over z_hi, y, core).
Axes of the slice: x: 4, y: 4, z: 8 (z_hi: 4, z_lo: 2; z = z_hi * 2 + z_lo), core: 2. Of those that a mesh axis runs over, the one named last changes fastest.
Arguments:
- counts: int32 [8], P('replica'), may hold values from 100 to 1000
- inner: bfloat16 [8, 3, 2, 8192, 1024], P('replica', None, None, 'fsdp'), may hold values from -6 to 6
- anchor: bfloat16 [3, 2, 8192, 1024], P(None, None, 'fsdp'), may hold values from -6 to 6
- momentum: float32 [3, 2, 8192, 1024], P(None, None, ('fsdp', 'replica')), may hold values from -6 to 6
Outputs:
- new_weights: bfloat16 [3, 2, 8192, 1024], P(None, None, 'fsdp')
- new_momentum: float32 [3, 2, 8192, 1024], P(None, None, ('fsdp', 'replica'))
Inputs may be any that keep to these rules, and one draw needn't show every extreme that they name: `counts`: inner steps of a group.
All inputs are finite; a program needn't handle non-finite values.
Results may differ from a plain program's by a relative error of at most 0.001.
Values may be sent and summed in bfloat16 or wider, within the bound.
A program may use at most 128 MiB of HBM per device.

v0:
```python
import jax
import jax.numpy as jnp
from jax import lax
from jax.sharding import PartitionSpec as P

LAYERS = 3
outer_rate = 0.7
momentum_rate = 0.9


def on_device(counts, inner, anchor, momentum):
    total = lax.psum(counts[0], "replica").astype(jnp.float32)
    share = counts[0].astype(jnp.float32) / total
    owned_rows = momentum.shape[2]
    start = lax.axis_index("replica") * owned_rows
    weight_list = []
    moment_list = []
    for layer in range(LAYERS):
        base = anchor[layer].astype(jnp.float32)
        term = share * (base - inner[0, layer].astype(jnp.float32))
        pseudo = lax.psum(term, "replica")
        moment_full = lax.all_gather(momentum[layer], "replica", axis=1, tiled=True)
        moment_next = momentum_rate * moment_full + pseudo
        weights_next = (base - outer_rate * (pseudo + momentum_rate * moment_next)).astype(
            jnp.bfloat16
        )
        moment_list.append(lax.dynamic_slice_in_dim(moment_next, start, owned_rows, 1))
        weight_list.append(weights_next)
    return (jnp.stack(weight_list), jnp.stack(moment_list))


def solution(mesh):
    placed = (
        P("replica"),
        P("replica", None, None, "fsdp", None),
        P(None, None, "fsdp", None),
        P(None, None, ("fsdp", "replica"), None),
    )
    return jax.shard_map(
        on_device,
        mesh=mesh,
        in_specs=placed,
        out_specs=(P(None, None, "fsdp", None), P(None, None, ("fsdp", "replica"), None)),
        check_vma=False,
    )
```

profile of v0, /device:TPU:8, one launch (start us, length us, event | category | flops | bytes accessed | tf_op | source)
XLA Modules:
  0.0 314.4 jit_solution(1849387459540233903)
XLA Ops:
  7.2 0.0 all-gather.11.cloned.1.call-start
  7.2 2.0 fusion.9
  9.2 0.0 all-gather.11.cloned.1.call-update
  9.2 0.0 all-reduce.3.cloned.1.call-start
  9.3 13.1 %psum.28 = s32[]{:T(128)} all-reduce(s32[]{:T(128)} %bitcast.1), channel_id=1, replica_groups=mesh['replica'=8,'fsdp'=32] {'replica'}, use_global_device_ids=true, to_apply=%region_0.0 | all-reduce | flops 1 | bytes 8 | tf_op jit(solution)/shard_map/psum | solution.py:12
  23.8 6.1 %fusion = (f32[2,256,1024]{2,1,0:T(8,128)}, f32[2,256,1024]{2,1,0:T(8,128)}, f32[2,256,1024]{2,1,0:T(8,128)}) fusion(bf16[1,3,2,256,1024]{4,3,2,1,0:T(8,128)(2,1)} %param.5, f32[]{:T(128)S(6)} %div.3, bf16[3,2,256,1024]{3,2,1,0:T(8,128)(2,1)} %param.6), kind=kLoop, calls=%fused_computation.7 | loop fusion | flops 6291456 | bytes 12582916 | tf_op jit(solution)/shard_map/mul | solution.py:20
  29.9 0.0 all-reduce.3.cloned.1.call-update
  29.9 0.0 all-gather.9.cloned.1.call-start
  30.0 0.7 all-gather.9.cloned.1.call-update
  30.7 0.0 all-gather.7.cloned.1.call-start
  30.7 0.5 all-gather.7.cloned.1.call-update
  31.3 25.7 %all-gather.11.cloned.1.call-done = f32[1,2,256,1024]{3,2,1,0:T(8,128)} async-done(((f32[1,2,32,1024]{3,2,1,0:T(8,128)}), f32[1,2,256,1024]{3,2,1,0:T(8,128)}) %all-gather.11.cloned.1.call-update) | async-done | bytes 2097168 | tf_op jit(solution)/shard_map/all_gather | solution.py:22
  57.0 153.2 %all-reduce.3.cloned.1.call-done = (f32[2,256,1024]{2,1,0:T(8,128)}, f32[2,256,1024]{2,1,0:T(8,128)}, f32[2,256,1024]{2,1,0:T(8,128)}) async-done(((f32[2,256,1024]{2,1,0:T(8,128)}, f32[2,256,1024]{2,1,0:T(8,128)}, f32[2,256,1024]{2,1,0:T(8,128)}), (f32[2,256,1024]{2,1,0:T(8,128)}, f32[2,256,1024]{2,1,0:T(8,128)}, f32[2,256,1024]{2,1,0:T(8,128)})) %all-reduce.3.cloned.1.call-update) | async-done | bytes 6291472 | tf_op jit(solution)/shard_map/psum | solution.py:21
  210.2 3.8 %bitcast_add_fusion = (f32[2,256,1024]{2,1,0:T(8,128)S(1)}, bf16[1,2,256,1024]{3,2,1,0:T(8,128)(2,1)}) fusion(f32[2,256,1024]{2,1,0:T(8,128)} %get-tuple-element.2, f32[1,2,256,1024]{3,2,1,0:T(8,128)} %all-gather.11.cloned.1.call-done, bf16[3,2,256,1024]{3,2,1,0:T(8,128)(2,1)S(1)} %copy-done), kind=kLoop, calls=%fused_computation.13 | loop fusion | flops 4194304 | bytes 8388608 | tf_op jit(solution)/shard_map/add | solution.py:23
  214.1 41.2 %all-gather.9.cloned.1.call-done = f32[1,2,256,1024]{3,2,1,0:T(8,128)} async-done(((f32[1,2,32,1024]{3,2,1,0:T(8,128)}), f32[1,2,256,1024]{3,2,1,0:T(8,128)}) %all-gather.9.cloned.1.call-update) | async-done | bytes 2097168 | tf_op jit(solution)/shard_map/all_gather | solution.py:22
  255.3 3.9 %bitcast_add_fusion.1 = (f32[2,256,1024]{2,1,0:T(8,128)S(1)}, bf16[1,2,256,1024]{3,2,1,0:T(8,128)(2,1)}) fusion(f32[2,256,1024]{2,1,0:T(8,128)} %get-tuple-element.3, f32[1,2,256,1024]{3,2,1,0:T(8,128)} %all-gather.9.cloned.1.call-done, bf16[3,2,256,1024]{3,2,1,0:T(8,128)(2,1)S(1)} %copy-done), kind=kLoop, calls=%fused_computation.14 | loop fusion | flops 4194304 | bytes 8388608 | tf_op jit(solution)/shard_map/add | solution.py:23
  259.1 0.7 dynamic-slice_bitcast_fusion.1
  259.9 41.0 %all-gather.7.cloned.1.call-done = f32[1,2,256,1024]{3,2,1,0:T(8,128)} async-done(((f32[1,2,32,1024]{3,2,1,0:T(8,128)}), f32[1,2,256,1024]{3,2,1,0:T(8,128)}) %all-gather.7.cloned.1.call-update) | async-done | bytes 2097168 | tf_op jit(solution)/shard_map/all_gather | solution.py:22
  300.9 3.1 bitcast_add_fusion.2
  304.0 0.0 copy-start.1
  304.1 0.9 pad_maximum_fusion.1
  305.0 0.5 copy-done.1
  305.5 0.3 copy-done.2
  305.8 2.0 pad_maximum_fusion
  (7 shorter events, 0.1 us)
Async XLA Ops:
  7.2 49.8 %all-gather.11.cloned.1.call-start = ((), (), s32[]{:S(2)}) async-start(), calls=%async_computation.2 | async-start | bytes 2359296 | tf_op jit(solution)/shard_map/all_gather | solution.py:22
  9.2 201.0 %all-reduce.3.cloned.1.call-start = ((), (), s32[]{:S(2)}) async-start(), calls=%async_computation.3 | async-start | bytes 12582912 | tf_op jit(solution)/shard_map/psum | solution.py:21
  29.9 180.3 %copy-start = (bf16[3,2,256,1024]{3,2,1,0:T(8,128)(2,1)S(1)}, bf16[3,2,256,1024]{3,2,1,0:T(8,128)(2,1)}, u32[]{:S(2)}) copy-start(bf16[3,2,256,1024]{3,2,1,0:T(8,128)(2,1)} %param.6) | copy-start | bytes 9437188
  29.9 225.3 %all-gather.9.cloned.1.call-start = ((), (), s32[]{:S(2)}) async-start(), calls=%async_computation.1 | async-start | bytes 2359296 | tf_op jit(solution)/shard_map/all_gather | solution.py:22
  30.7 270.2 %all-gather.7.cloned.1.call-start = ((), (), s32[]{:S(2)}) async-start(), calls=%async_computation | async-start | bytes 2359296 | tf_op jit(solution)/shard_map/all_gather | solution.py:22
  300.9 3.2 %copy-start.3 = (f32[1,2,32,1024]{3,2,1,0:T(8,128)S(1)}, f32[1,2,32,1024]{3,2,1,0:T(8,128)}, u32[]{:S(2)}) copy-start(f32[1,2,32,1024]{3,2,1,0:T(8,128)} %dynamic-slice_bitcast_fusion.1) | copy-start | bytes 786436
  304.0 1.5 copy-start.1
  304.0 1.8 copy-start.2
Sparse Core Ops, SparseCore 0:
  9.8 47.1 all-gather.10
  60.5 149.7 all-reduce.2
  212.0 43.1 all-gather.8
  257.5 43.3 all-gather.6
where the time goes:
time: 315 us; the launch traced here: 314 us
  waiting for transfers between devices  262 us (83%)
  other arithmetic  19.9 us (6%)
  between operations  15.2 us (5%)
  blocking collectives  13.1 us (4%)
  local copies, waits for them, and re-layouts  3.61 us (1%)
    psum x1, waiting for transfers between devices, on_device(): pseudo = lax.psum(term, 'replica')  153 us
    all_gather x3, waiting for transfers between devices, on_device(): moment_full = lax.all_gather(momentum[layer], 'replica', axis=1, tiled=True)  108 us
    psum x1, blocking collectives, on_device(): total = lax.psum(counts[0], 'replica').astype(jnp.float32)  13.1 us
    add x3, other arithmetic, on_device(): moment_next = momentum_rate * moment_full + pseudo  10.8 us
  transfers between devices with their start and end apart: 4, of which 4 were waited for; matrix products, arithmetic and copies ran while one was open for 5% of the time, Pallas kernels for 0%

commit v1 on v0

--- a/solution.py
+++ b/solution.py
@@ -18,7 +18,7 @@
     for layer in range(LAYERS):
         base = anchor[layer].astype(jnp.float32)
         term = share * (base - inner[0, layer].astype(jnp.float32))
-        pseudo = lax.psum(term, "replica")
+        pseudo = jnp.sum(lax.all_gather(term, "replica"), axis=0)
         moment_full = lax.all_gather(momentum[layer], "replica", axis=1, tiled=True)
         moment_next = momentum_rate * moment_full + pseudo
         weights_next = (base - outer_rate * (pseudo + momentum_rate * moment_next)).astype(

time: 315 us -> 699 us (2.22)
  waiting for transfers between devices: 262 us -> 619 us
  other arithmetic: 19.9 us -> 47.9 us
    all_gather x0 -> x3, waiting for transfers between devices: none -> 499 us  [on_device(): pseudo = jnp.sum(lax.all_gather(term, 'replica'), axis=0)]
    psum x1 -> x0, waiting for transfers between devices: 153 us -> none  [on_device(): pseudo = lax.psum(term, 'replica')]
    reduce_sum x0 -> x3, other arithmetic: none -> 27.9 us  [on_device(): pseudo = jnp.sum(lax.all_gather(term, 'replica'), axis=0)]
    all_gather x3, waiting for transfers between devices: 108 us -> 118 us  [on_device(): moment_full = lax.all_gather(momentum[layer], 'replica', axis=1, tiled=True)]
  transfers between devices with their start and end apart: 4 -> 6, of which waited for: 4 -> 6; matrix products, arithmetic and copies ran while one was open for 5% -> 5% of each run, Pallas kernels for 0% -> 0%
where the time goes in v1:
time: 699 us; the launch traced here: 698 us
  waiting for transfers between devices  619 us (89%)
  other arithmetic  47.9 us (7%)
  between operations  15.5 us (2%)
  blocking collectives  13 us (2%)
    all_gather x3, waiting for transfers between devices, on_device(): pseudo = jnp.sum(lax.all_gather(term, 'replica'), axis=0)  499 us
    all_gather x3, waiting for transfers between devices, on_device(): moment_full = lax.all_gather(momentum[layer], 'replica', axis=1, tiled=True)  118 us
    reduce_sum x3, other arithmetic, on_device(): pseudo = jnp.sum(lax.all_gather(term, 'replica'), axis=0)  27.9 us
  transfers between devices with their start and end apart: 6, of which 6 were waited for; matrix products, arithmetic and copies ran while one was open for 5% of the time, Pallas kernels for 0%

profile of v1, /device:TPU:8, one launch (start us, length us, event | category | flops | bytes accessed | tf_op | source)
XLA Modules:
  0.0 698.4 jit_solution(35592414746616576)
XLA Ops:
  7.9 13.0 %psum.7 = s32[]{:T(128)} all-reduce(s32[]{:T(128)} %bitcast.1), channel_id=1, replica_groups=mesh['replica'=8,'fsdp'=32] {'replica'}, use_global_device_ids=true, to_apply=%region_0.0 | all-reduce | flops 1 | bytes 8 | tf_op jit(solution)/shard_map/psum | solution.py:12
  21.6 6.2 fusion.2
  27.9 0.7 all-gather.12.cloned.1.call-update
  28.6 0.7 all-gather.10.cloned.1.call-update
  29.4 0.9 fusion.12
  30.3 0.5 all-gather.18.cloned.1.call-update
  30.9 0.5 all-gather.16.cloned.1.call-update
  31.4 169.7 %all-gather.14.cloned.1.call-done = f32[8,2,256,1024]{3,2,1,0:T(8,128)} async-done(((f32[1,2,256,1024]{3,2,1,0:T(8,128)}), f32[8,2,256,1024]{3,2,1,0:T(8,128)}) %all-gather.14.cloned.1.call-update) | async-done | bytes 16777232 | tf_op jit(solution)/shard_map/all_gather | solution.py:21
  201.2 9.4 %reduce_sum.29 = f32[2,256,1024]{2,1,0:T(8,128)} reduce(f32[8,2,256,1024]{3,2,1,0:T(8,128)} %all-gather.14.cloned.1.call-done, f32[]{:T(128)} %constant.2.clone.1), dimensions={0}, to_apply=%region_3.0 | reduce | flops 3670016 | bytes 18874372 | tf_op jit(solution)/shard_map/reduce_sum | solution.py:21
  210.5 164.4 %all-gather.12.cloned.1.call-done = f32[8,2,256,1024]{3,2,1,0:T(8,128)} async-done(((f32[1,2,256,1024]{3,2,1,0:T(8,128)}), f32[8,2,256,1024]{3,2,1,0:T(8,128)}) %all-gather.12.cloned.1.call-update) | async-done | bytes 16777232 | tf_op jit(solution)/shard_map/all_gather | solution.py:21
  374.9 9.3 %reduce_sum.28 = f32[2,256,1024]{2,1,0:T(8,128)} reduce(f32[8,2,256,1024]{3,2,1,0:T(8,128)} %all-gather.12.cloned.1.call-done, f32[]{:T(128)} %constant.2.clone.1), dimensions={0}, to_apply=%region_2.0 | reduce | flops 3670016 | bytes 18874372 | tf_op jit(solution)/shard_map/reduce_sum | solution.py:21
  384.2 165.0 %all-gather.10.cloned.1.call-done = f32[8,2,256,1024]{3,2,1,0:T(8,128)} async-done(((f32[1,2,256,1024]{3,2,1,0:T(8,128)}), f32[8,2,256,1024]{3,2,1,0:T(8,128)}) %all-gather.10.cloned.1.call-update) | async-done | bytes 16777232 | tf_op jit(solution)/shard_map/all_gather | solution.py:21
  549.2 9.3 %reduce_sum.27 = f32[2,256,1024]{2,1,0:T(8,128)} reduce(f32[8,2,256,1024]{3,2,1,0:T(8,128)} %all-gather.10.cloned.1.call-done, f32[]{:T(128)} %constant.2.clone.1), dimensions={0}, to_apply=%region_1.0 | reduce | flops 3670016 | bytes 18874372 | tf_op jit(solution)/shard_map/reduce_sum | solution.py:21
  558.5 35.5 %all-gather.20.cloned.1.call-done = f32[1,2,256,1024]{3,2,1,0:T(8,128)} async-done(((f32[1,2,32,1024]{3,2,1,0:T(8,128)}), f32[1,2,256,1024]{3,2,1,0:T(8,128)}) %all-gather.20.cloned.1.call-update) | async-done | bytes 2097168 | tf_op jit(solution)/shard_map/all_gather | solution.py:22
  594.0 3.9 bitcast_add_fusion
  597.9 41.1 %all-gather.18.cloned.1.call-done = f32[1,2,256,1024]{3,2,1,0:T(8,128)} async-done(((f32[1,2,32,1024]{3,2,1,0:T(8,128)}), f32[1,2,256,1024]{3,2,1,0:T(8,128)}) %all-gather.18.cloned.1.call-update) | async-done | bytes 2097168 | tf_op jit(solution)/shard_map/all_gather | solution.py:22
  639.0 3.9 bitcast_add_fusion.1
  642.9 0.7 dynamic-slice_bitcast_fusion.1
  643.6 41.0 %all-gather.16.cloned.1.call-done = f32[1,2,256,1024]{3,2,1,0:T(8,128)} async-done(((f32[1,2,32,1024]{3,2,1,0:T(8,128)}), f32[1,2,256,1024]{3,2,1,0:T(8,128)}) %all-gather.16.cloned.1.call-update) | async-done | bytes 2097168 | tf_op jit(solution)/shard_map/all_gather | solution.py:22
  684.7 3.1 bitcast_add_fusion.2
  687.8 0.9 pad_maximum_fusion.1
  688.8 0.5 copy-done.1
  689.3 0.3 copy-done.2
  689.6 2.0 pad_maximum_fusion
  (18 shorter events, 0.3 us)
Async XLA Ops:
  7.2 194.0 %all-gather.14.cloned.1.call-start = ((), (), s32[]{:S(2)}) async-start(), calls=%async_computation.2 | async-start | bytes 18874368 | tf_op jit(solution)/shard_map/all_gather | solution.py:21
  27.8 347.1 %all-gather.12.cloned.1.call-start = ((), (), s32[]{:S(2)}) async-start(), calls=%async_computation.1 | async-start | bytes 18874368 | tf_op jit(solution)/shard_map/all_gather | solution.py:21
  27.9 1.5 copy-start.4
  28.6 520.7 %all-gather.10.cloned.1.call-start = ((), (), s32[]{:S(2)}) async-start(), calls=%async_computation | async-start | bytes 18874368 | tf_op jit(solution)/shard_map/all_gather | solution.py:21
  29.3 564.7 %all-gather.20.cloned.1.call-start = ((), (), s32[]{:S(2)}) async-start(), calls=%async_computation.5 | async-start | bytes 2359296 | tf_op jit(solution)/shard_map/all_gather | solution.py:22
  30.3 608.8 %all-gather.18.cloned.1.call-start = ((), (), s32[]{:S(2)}) async-start(), calls=%async_computation.4 | async-start | bytes 2359296 | tf_op jit(solution)/shard_map/all_gather | solution.py:22
  30.9 653.8 %all-gather.16.cloned.1.call-start = ((), (), s32[]{:S(2)}) async-start(), calls=%async_computation.3 | async-start | bytes 2359296 | tf_op jit(solution)/shard_map/all_gather | solution.py:22
  384.2 209.8 %copy-start = (bf16[3,2,256,1024]{3,2,1,0:T(8,128)(2,1)S(1)}, bf16[3,2,256,1024]{3,2,1,0:T(8,128)(2,1)}, u32[]{:S(2)}) copy-start(bf16[3,2,256,1024]{3,2,1,0:T(8,128)(2,1)} %param.6) | copy-start | bytes 9437188
  684.7 3.2 copy-start.3
  687.8 1.5 copy-start.1
  687.8 1.8 copy-start.2
Sparse Core Ops, SparseCore 0:
  27.9 173.2 all-gather.13
  203.0 171.8 all-gather.11
  377.3 171.8 all-gather.9
  550.9 43.0 all-gather.19
  595.6 43.3 all-gather.17
  641.3 43.3 all-gather.15
